TPU v7x, 128 devices: a whole 4x4x4 slice. The times are simulated.
128 devices in a mesh: grp: 4 (over x_hi, core), sub: 32 (over x_lo, y, z).
Axes of the slice: x: 4 (x_hi: 2, x_lo: 2; x = x_hi * 2 + x_lo), y: 4, z: 4, core: 2. Of those that a mesh axis runs over, the one named last changes fastest.
Arguments:
- template: bfloat16 [96, 96, 128], P('sub'), may hold values from -4 to 4
- subjects: bfloat16 [128, 96, 96, 128], P(('grp', 'sub')), may hold values from -40 to 40
Outputs:
- velocity: float32 [96, 3, 96, 128], P('sub')
- new_template: float32 [96, 96, 128], P('sub')
- similarity: float32 [], replicated
All inputs are finite; a program needn't handle non-finite values.
Results may differ from a plain program's by a relative error of at most 0.0003.
Values may be sent and summed in bfloat16 or wider, within the bound.
No kernel may reach another device: no remote copies, remote signals or barrier semaphores. Data moves between devices by JAX's collectives and lax.ppermute only.
A program may use at most 128 MiB of HBM per device.

v0:
```python
import math
import jax
import jax.numpy as jnp
from jax import lax
from jax.sharding import PartitionSpec as P

RADIUS = 4
REACH = 5
EPSILON = 1e-05
STEP_LENGTH = 0.5
VARIANCE = 3.0
HIGH = lax.Precision.HIGHEST


def padded_2(x, sides, width):
    for axis, dim in sides:
        devices, length = (lax.axis_size(axis), x.shape[dim])
        up = [(i, (i + 1) % devices) for i in range(devices - 1)]
        down = [(j, i) for i, j in up]
        last = lax.slice_in_dim(x, length - width, length, axis=dim)
        initial = lax.slice_in_dim(x, 0, width, axis=dim)
        before = lax.ppermute(last, axis, up)
        after = lax.ppermute(initial, axis, down)
        x = jnp.concatenate([before, x, after], axis=dim)
    return x


def band_matrix(length, extent, weighted):
    row_ids = lax.broadcasted_iota(jnp.int32, (length, length), 0)
    col_ids = lax.broadcasted_iota(jnp.int32, (length, length), 1)
    inside = jnp.abs(row_ids - col_ids) <= extent
    if weighted:
        kernel_sum = sum(
            (math.exp(-offset * offset / (2.0 * VARIANCE)) for offset in range(-extent, extent + 1))
        )
        offset_f = (row_ids - col_ids).astype(jnp.float32)
        values = jnp.exp(-offset_f * offset_f / (2.0 * VARIANCE)) / kernel_sum
        return jnp.where(inside, values, 0.0)
    return jnp.where(inside, 1.0 / (2 * extent + 1), 0.0).astype(jnp.float32)


def filter_volume(volume, along_z, along_x, along_y):
    result = jnp.dot(volume, along_y, precision=HIGH, preferred_element_type=jnp.float32)
    result = jnp.einsum(
        "ab,zby->zay", along_x, result, precision=HIGH, preferred_element_type=jnp.float32
    )
    return jnp.einsum(
        "ab,bxy->axy", along_z, result, precision=HIGH, preferred_element_type=jnp.float32
    )


def central(volume):
    padded = jnp.pad(volume, 1)
    along_z = (padded[2:, 1:-1, 1:-1] - padded[:-2, 1:-1, 1:-1]) * 0.5
    along_x = (padded[1:-1, 2:, 1:-1] - padded[1:-1, :-2, 1:-1]) * 0.5
    along_y = (padded[1:-1, 1:-1, 2:] - padded[1:-1, 1:-1, :-2]) * 0.5
    return jnp.stack([along_z, along_x, along_y], axis=1)


def on_device(template, subjects):
    fixed_image = lax.all_gather(template, "sub", axis=0, tiled=True).astype(jnp.float32)
    depth, height, width = fixed_image.shape
    box_z = band_matrix(depth, RADIUS, False)
    box_x = band_matrix(height, RADIUS, False)
    box_y = band_matrix(width, RADIUS, False)
    gauss_z = band_matrix(depth, REACH, True)
    gauss_x = band_matrix(height, REACH, True)
    gauss_y = band_matrix(width, REACH, True)
    mean_i = filter_volume(fixed_image, box_z, box_x, box_y)
    mean_ii = filter_volume(fixed_image * fixed_image, box_z, box_x, box_y)
    var_i = mean_ii - mean_i * mean_i
    centred_i = fixed_image - mean_i
    gradients = central(fixed_image)
    moving = subjects[0].astype(jnp.float32)
    mean_j = filter_volume(moving, box_z, box_x, box_y)
    mean_jj = filter_volume(moving * moving, box_z, box_x, box_y)
    mean_ij = filter_volume(fixed_image * moving, box_z, box_x, box_y)
    cross_sum = mean_ij - mean_i * mean_j
    var_j = mean_jj - mean_j * mean_j
    denominator = var_i * var_j + EPSILON
    factor = (
        2.0
        * cross_sum
        / denominator
        * (moving - mean_j - cross_sum / (var_i + EPSILON) * centred_i)
    )
    force_total = factor[:, None] * gradients
    cc_local = jnp.sum(cross_sum * cross_sum / denominator)
    planar = jnp.einsum(
        "zcxb,ba->zcxa", force_total, gauss_y, precision=HIGH, preferred_element_type=jnp.float32
    )
    planar = jnp.einsum(
        "ab,zcby->zcay", gauss_x, planar, precision=HIGH, preferred_element_type=jnp.float32
    )
    group_count = lax.axis_size("grp")
    subject_count = subjects.shape[0] * group_count * lax.axis_size("sub")
    smooth = jnp.einsum(
        "ab,bcxy->acxy", gauss_z, planar, precision=HIGH, preferred_element_type=jnp.float32
    )
    intensity = moving[:, None]
    owner_part = lax.psum_scatter(
        jnp.concatenate([smooth, intensity], axis=1), "sub", scatter_dimension=0, tiled=True
    )
    summed = lax.psum(owner_part, "grp")
    mean_velocity = summed[:, :3] / subject_count
    mean_image = summed[:, 3] / subject_count
    padded_mean = padded_2(mean_image, (("sub", 0),), 1)
    velocity_square = jnp.sum(mean_velocity * mean_velocity)
    image_square = jnp.sum(mean_image * mean_image)
    cc_total = lax.psum(cc_local, ("grp", "sub"))
    velocity_total, image_sq_total = lax.psum((velocity_square, image_square), "sub")
    cell_count = depth * height * width
    velocity_norm = jnp.sqrt(velocity_total / cell_count + EPSILON)
    image_norm = jnp.sqrt(image_sq_total / cell_count + EPSILON)
    velocity = STEP_LENGTH * mean_velocity / velocity_norm
    slope_z = (padded_mean[2:] - padded_mean[:-2]) * 0.5
    padded_x = jnp.pad(mean_image, ((0, 0), (1, 1), (0, 0)))
    slope_x = (padded_x[:, 2:] - padded_x[:, :-2]) * 0.5
    padded_y = jnp.pad(mean_image, ((0, 0), (0, 0), (1, 1)))
    slope_y = (padded_y[:, :, 2:] - padded_y[:, :, :-2]) * 0.5
    advected = velocity[:, 0] * slope_z + velocity[:, 1] * slope_x + velocity[:, 2] * slope_y
    new_template = (mean_image - advected) / image_norm
    similarity = cc_total / (subject_count * cell_count)
    return (velocity, new_template, similarity)


def solution(mesh):
    placed = (P("sub", None, None), P(("grp", "sub"), None, None, None))
    return jax.shard_map(
        on_device,
        mesh=mesh,
        in_specs=placed,
        out_specs=(P("sub", None, None, None), P("sub", None, None), P()),
        check_vma=False,
    )
```

profile of v0, /device:TPU:2, one launch (start us, length us, event | category | flops | bytes accessed | tf_op | source)
XLA Modules:
  0.0 771.6 jit_solution(3366972188630262749)
XLA Ops:
  13.9 6.3 copy.25
  20.1 9.0 %convolution_bitcast_fusion.1 = f32[96,96,128]{1,0,2:T(8,128)} fusion(f32[96,96,128]{1,0,2:T(8,128)} %copy.25), kind=kOutput, calls=%fused_computation.45 | convolution fusion | flops 1358991360 | bytes 9437184 | tf_op jit(solution)/shard_map/ab,zby->zay/dot_general | solution.py:44
  29.1 6.4 copy.26
  45.3 118.9 %all-gather.2.cloned.1.call-done = bf16[96,96,128]{2,1,0:T(8,128)(2,1)} async-done(((bf16[3,96,128]{2,1,0:T(8,128)(2,1)}), bf16[96,96,128]{2,1,0:T(8,128)(2,1)}) %all-gather.2.cloned.1.call-update) | async-done | bytes 2359312 | tf_op jit(solution)/shard_map/all_gather | solution.py:61
  168.1 7.6 fusion.17
  180.8 9.9 %fusion.15 = f32[96,96,128]{2,0,1:T(8,128)} fusion(f32[96,96,128]{2,1,0:T(8,128)S(1)} %convolution_bitcast_fusion.3), kind=kOutput, calls=%fused_computation.27 | convolution fusion | flops 1358991360 | bytes 9437184 | tf_op jit(solution)/shard_map/ab,bxy->axy/dot_general | solution.py:47
  190.7 7.6 fusion.21
  203.2 9.9 %fusion.19 = f32[96,96,128]{2,0,1:T(8,128)} fusion(f32[96,96,128]{2,1,0:T(8,128)S(1)} %convolution_bitcast_fusion.4), kind=kOutput, calls=%fused_computation.31 | convolution fusion | flops 1358991360 | bytes 9437184 | tf_op jit(solution)/shard_map/ab,bxy->axy/dot_general | solution.py:47
  213.1 7.6 fusion.25
  220.6 6.1 convolution_bitcast_fusion.6
  230.4 6.3 copy.22
  236.7 9.0 %convolution_bitcast_fusion.2 = f32[96,96,128]{1,0,2:T(8,128)} fusion(f32[96,96,128]{1,0,2:T(8,128)} %copy.22), kind=kOutput, calls=%fused_computation.46 | convolution fusion | flops 1358991360 | bytes 9437184 | tf_op jit(solution)/shard_map/ab,zby->zay/dot_general | solution.py:44
  245.7 6.3 copy.23
  251.9 8.8 %fusion.84 = f32[96,96,128]{2,0,1:T(8,128)} fusion(f32[96,96,128]{2,0,1:T(8,128)} %copy.23), kind=kOutput, calls=%fused_computation.118 | convolution fusion | flops 1358991360 | bytes 9437184 | tf_op jit(solution)/shard_map/ab,bxy->axy/dot_general | solution.py:47
  261.5 7.5 fusion.8
  269.0 21.9 %fusion.27 = (f32[]{:T(128)}, f32[96,96,128]{2,0,1:T(8,128)}) fusion(f32[96,96,128]{2,0,1:T(8,128)} %fusion.84, f32[96,96,128]{2,0,1:T(8,128)} %fusion.81, f32[96,96,128]{2,0,1:T(8,128)} %fusion.15, f32[96,96,128]{2,0,1:T(8,128)} %fusion.19, bf16[96,96,128]{2,1,0:T(8,128)(2,1)S(1)} %copy-done.2, bf16[1,96,96,128]{3,2,1,0:T(8,128)(2,1)S(1)} %copy-done, ...), kind=kOutput, calls=%fused_computation.43 | convolution fusion | flops 1384943616 | bytes 33030148 | tf_op jit(solution)/shard_map/ab,bxy->axy/dot_general | solution.py:47
  296.1 22.1 %fusion.2 = f32[96,3,96,128]{3,2,1,0:T(8,128)S(1)} fusion(f32[96,3,96,128]{3,0,2,1:T(8,128)S(1)} %maximum_multiply_fusion), kind=kOutput, calls=%fused_computation.10 | convolution fusion | flops 5435965440 | bytes 28311552 | tf_op jit(solution)/shard_map/zcxb,ba->zcxa/dot_general | solution.py:89
  318.2 15.9 %convolution_bitcast_fusion = f32[96,3,96,128]{3,2,1,0:T(8,128)} fusion(f32[96,3,96,128]{3,2,1,0:T(8,128)S(1)} %fusion.2), kind=kOutput, calls=%fused_computation.12 | convolution fusion | flops 4076946432 | bytes 28311552 | tf_op jit(solution)/shard_map/ab,zcby->zcay/dot_general | solution.py:92
  334.1 25.3 %fusion = f32[96,3,96,128]{3,0,2,1:T(8,128)S(1)} fusion(f32[96,3,96,128]{3,2,1,0:T(8,128)} %convolution_bitcast_fusion), kind=kOutput, calls=%fused_computation.8 | convolution fusion | flops 4076946432 | bytes 28311552 | tf_op jit(solution)/shard_map/ab,bcxy->acxy/dot_general | solution.py:97
  359.5 7.1 pad_maximum_fusion
  366.6 15.8 %copy.34 = f32[96,4,96,128]{3,2,1,0:T(8,128)} copy(f32[96,4,96,128]{3,0,2,1:T(8,128)} %pad_maximum_fusion) | data formatting | bytes 37748736 | tf_op jit(solution)/shard_map/concatenate | solution.py:102
  382.4 218.4 %reduce-scatter.2.cloned.1.call-done = f32[3,4,96,128]{3,2,1,0:T(8,128)} async-done(((f32[96,4,96,128]{3,2,1,0:T(8,128)}), f32[3,4,96,128]{3,2,1,0:T(8,128)}) %reduce-scatter.2.cloned.1.call-update) | async-done | bytes 589840 | tf_op jit(solution)/shard_map/reduce_scatter | solution.py:101
  600.9 64.6 %psum.31 = f32[]{:T(128)} all-reduce(f32[]{:T(128)} %get-tuple-element.14), channel_id=1, replica_groups=mesh['grp'=4,'sub'=32] {'grp','sub'}, use_global_device_ids=true, to_apply=%region_7.8 | all-reduce | flops 1 | bytes 8 | tf_op jit(solution)/shard_map/psum | solution.py:110
  669.4 79.7 %all-reduce.3 = (f32[]{:T(128)}, f32[]{:T(128)}) all-reduce(f32[]{:T(128)} %multiply_reduce_fusion, f32[]{:T(128)} %multiply_reduce_fusion.1), channel_id=1, replica_groups=mesh['grp'=4,'sub'=32] {'sub'}, use_global_device_ids=true, to_apply=%region_3.4 | all-reduce | flops 2 | bytes 16 | tf_op jit(solution)/shard_map/psum | solution.py:111
  (44 shorter events, 56.6 us)
Async XLA Ops:
  7.2 157.0 %all-gather.2.cloned.1.call-start = ((), (), s32[]{:S(2)}) async-start(), calls=%async_computation.1 | async-start | bytes 2433024 | tf_op jit(solution)/shard_map/all_gather | solution.py:61
  7.9 592.9 %reduce-scatter.2.cloned.1.call-start = ((), (), s32[]{:S(2)}) async-start(), calls=%async_computation.2 | async-start | bytes 19464192 | tf_op jit(solution)/shard_map/reduce_scatter | solution.py:101
  29.1 6.4 copy-start
  35.5 3.9 copy-start.3
  220.6 6.2 copy-start.1
  251.9 8.8 %copy-start.2 = (bf16[96,96,128]{2,1,0:T(8,128)(2,1)S(1)}, bf16[96,96,128]{2,1,0:T(8,128)(2,1)}, u32[]{:S(2)}) copy-start(bf16[96,96,128]{2,1,0:T(8,128)(2,1)} %all-gather.2.cloned.1.call-done) | copy-start | bytes 7077892
  269.0 21.9 %copy-start.4 = (f32[96,1,96,128]{3,0,2,1:T(8,128)S(1)}, f32[96,1,96,128]{3,0,2,1:T(8,128)}, u32[]{:S(2)}) copy-start(f32[96,1,96,128]{3,0,2,1:T(8,128)} %get-tuple-element.16) | copy-start | bytes 14155780
  269.0 21.9 %copy-start.5 = (f32[96,1,96,128]{3,0,2,1:T(8,128)S(1)}, f32[96,1,96,128]{3,0,2,1:T(8,128)}, u32[]{:S(2)}) copy-start(f32[96,1,96,128]{3,0,2,1:T(8,128)} %get-tuple-element.17) | copy-start | bytes 14155780
  318.2 41.2 %slice-start = ((s8[4718592]{0:T(1024)(128)(4,1)}), s8[4194304]{0:T(1024)(128)(4,1)S(1)}, s32[]{:S(2)}) async-start(s8[4718592]{0:T(1024)(128)(4,1)} %bitcast.107), calls=%async_computation.4 | async-start | bytes 8388608
  334.1 25.3 %slice-start.1 = ((s8[4718592]{0:T(1024)(128)(4,1)}), s8[524288]{0:T(1024)(128)(4,1)S(1)}, s32[]{:S(2)}) async-start(s8[4718592]{0:T(1024)(128)(4,1)} %bitcast.107), calls=%async_computation.5 | async-start | bytes 1048576
  382.4 283.1 %all-reduce.6.cloned.1.call-start = ((), (), s32[]{:S(2)}) async-start(), calls=%async_computation.3 | async-start | bytes 1179648 | tf_op jit(solution)/shard_map/psum | solution.py:104
  750.7 8.4 %collective-permute-start = (f32[1,96,128]{2,1,0:T(8,128)S(1)}, f32[1,96,128]{2,1,0:T(8,128)S(1)}, u32[]{:S(2)}, u32[]{:S(2)}) collective-permute-start(f32[1,96,128]{2,1,0:T(8,128)S(1)} %get-tuple-element.24), channel_id=1, source_target_pairs={{1,0},{2,1},{3,2},{4,3},{5,4},{6,5},{7,6},{8,7},{9,8},{10,9},{11,1... | collective-permute-start | bytes 147464 | tf_op jit(solution)/shard_map/ppermute | solution.py:23
  752.7 10.2 %collective-permute-start.1 = (f32[1,96,128]{2,1,0:T(8,128)S(1)}, f32[1,96,128]{2,1,0:T(8,128)S(1)}, u32[]{:S(2)}, u32[]{:S(2)}) collective-permute-start(f32[1,96,128]{2,1,0:T(8,128)S(1)} %get-tuple-element.25), channel_id=1, source_target_pairs={{0,1},{1,2},{2,3},{3,4},{4,5},{5,6},{6,7},{7,8},{8,9},{9,10},{10,1... | collective-permute-start | bytes 147464 | tf_op jit(solution)/shard_map/ppermute | solution.py:22
Sparse Core Ops, SparseCore 0:
  9.6 154.5 all-gather.1
  382.5 218.3 reduce-scatter.1
  603.4 40.4 all-reduce.5
where the time goes:
time: 778 us; the launch traced here: 772 us
  waiting for transfers between devices  342 us (44%)
  matrix products  186 us (24%)
  blocking collectives  144 us (19%)
  local copies, waits for them, and re-layouts  42.6 us (5%)
  other arithmetic  33.7 us (4%)
  between operations  17.4 us (2%)
    reduce_scatter x1, waiting for transfers between devices, on_device(): lax.psum_scatter(jnp.concatenate([smooth, intensity], axis=1), 'sub', sca...  218 us
    all_gather x1, waiting for transfers between devices, on_device(): lax.all_gather(template, 'sub', axis=0, tiled=True).astype(jnp.float32)  119 us
    psum x1, blocking collectives, on_device(): lax.psum((velocity_square, image_square), 'sub')  79.7 us
    psum x1, blocking collectives, on_device(): cc_total = lax.psum(cc_local, ('grp', 'sub'))  64.6 us
    dot_general x5, matrix products, filter_volume(): jnp.einsum('ab,bxy->axy', along_z, result, precision=HIGH, preferred_elem...  56.4 us
    dot_general x5, matrix products, filter_volume(): jnp.einsum('ab,zby->zay', along_x, result, precision=HIGH, preferred_elem...  34.1 us
    dot_general x5, matrix products, filter_volume(): jnp.dot(volume, along_y, precision=HIGH, preferred_element_type=jnp.float32)  32.2 us
    dot_general x1, matrix products, on_device(): jnp.einsum('ab,bcxy->acxy', gauss_z, planar, precision=HIGH, preferred_el...  25.3 us
  transfers between devices with their start and end apart: 5, of which 3 were waited for; matrix products, arithmetic and copies ran while one was open for 5% of the time, Pallas kernels for 0%

commit v1 on v0

--- a/solution.py
+++ b/solution.py
@@ -58,7 +58,9 @@
 
 
 def on_device(template, subjects):
-    fixed_image = lax.all_gather(template, "sub", axis=0, tiled=True).astype(jnp.float32)
+    fixed_image = jnp.concatenate(
+        lax.all_to_all(jnp.stack([template] * lax.axis_size("sub")), "sub", 0, 0), axis=0
+    ).astype(jnp.float32)
     depth, height, width = fixed_image.shape
     box_z = band_matrix(depth, RADIUS, False)
     box_x = band_matrix(height, RADIUS, False)

time: 778 us -> 685 us (0.88)
  waiting for transfers between devices: 342 us -> 222 us
  other arithmetic: 33.7 us -> 45.4 us
  starting transfers between devices: 5.96 us -> 15.5 us
    all_gather x1 -> x0, waiting for transfers between devices: 119 us -> none  [on_device(): lax.all_gather(template, 'sub', axis=0, tiled=True).astype(jnp.float32)]
    all_to_all x0 -> x1, starting transfers between devices: none -> 9.57 us  [on_device(): lax.all_to_all(jnp.stack([template] * lax.axis_size('sub')), 'sub', 0, 0)]
    another operation x1, other arithmetic: 7.52 us -> 15.5 us  [central(): return jnp.stack([along_z, along_x, along_y], axis=1)]
  transfers between devices with their start and end apart: 5 -> 5, of which waited for: 3 -> 2; matrix products, arithmetic and copies ran while one was open for 5% -> 6% of each run, Pallas kernels for 0% -> 0%
where the time goes in v1:
time: 685 us; the launch traced here: 676 us
  waiting for transfers between devices  222 us (32%)
  matrix products  186 us (27%)
  blocking collectives  144 us (21%)
  other arithmetic  45.4 us (7%)
  local copies, waits for them, and re-layouts  44.4 us (6%)
  between operations  17.8 us (3%)
  starting transfers between devices  15.5 us (2%)
    reduce_scatter x1, waiting for transfers between devices, on_device(): lax.psum_scatter(jnp.concatenate([smooth, intensity], axis=1), 'sub', sca...  218 us
    psum x1, blocking collectives, on_device(): lax.psum((velocity_square, image_square), 'sub')  79.7 us
    psum x1, blocking collectives, on_device(): cc_total = lax.psum(cc_local, ('grp', 'sub'))  64.7 us
    dot_general x5, matrix products, filter_volume(): jnp.einsum('ab,bxy->axy', along_z, result, precision=HIGH, preferred_elem...  56.5 us
    dot_general x5, matrix products, filter_volume(): jnp.einsum('ab,zby->zay', along_x, result, precision=HIGH, preferred_elem...  34.1 us
    dot_general x5, matrix products, filter_volume(): jnp.dot(volume, along_y, precision=HIGH, preferred_element_type=jnp.float32)  32.5 us
    dot_general x1, matrix products, on_device(): jnp.einsum('ab,bcxy->acxy', gauss_z, planar, precision=HIGH, preferred_el...  25.3 us
    dot_general x1, matrix products, on_device(): jnp.einsum('zcxb,ba->zcxa', force_total, gauss_y, precision=HIGH, preferr...  22.1 us
  transfers between devices with their start and end apart: 5, of which 2 were waited for; matrix products, arithmetic and copies ran while one was open for 6% of the time, Pallas kernels for 0%

profile of v1, /device:TPU:2, one launch (start us, length us, event | category | flops | bytes accessed | tf_op | source)
XLA Modules:
  0.0 675.6 jit_solution(14704381296583876196)
XLA Ops:
  9.8 9.6 %all-to-all-start = ((bf16[32,3,96,128]{3,2,1,0:T(8,128)(2,1)}), bf16[32,3,96,128]{3,2,1,0:T(8,128)(2,1)S(1)}, u32[]{:S(2)}, u32[]{:S(2)}) async-start(bf16[32,3,96,128]{3,2,1,0:T(8,128)(2,1)} %stack.10), calls=%async_computation | async-start | bytes 4718592 | tf_op jit(solution)/shard_map/all_to_all | solution.py:62
  25.3 6.3 copy.26
  31.6 9.0 %convolution_bitcast_fusion.1 = f32[96,96,128]{1,0,2:T(8,128)} fusion(f32[96,96,128]{1,0,2:T(8,128)} %copy.26), kind=kOutput, calls=%fused_computation.45 | convolution fusion | flops 1358991360 | bytes 9437184 | tf_op jit(solution)/shard_map/ab,zby->zay/dot_general | solution.py:44
  40.6 6.3 copy.27
  68.0 7.6 %fusion.17 = f32[96,96,128]{2,1,0:T(8,128)S(1)} fusion(f32[96,96,128]{2,0,1:T(8,128)S(1)} %get-tuple-element.19), kind=kOutput, calls=%fused_computation.29 | convolution fusion | flops 1812004864 | bytes 9437184 | tf_op jit(solution)/shard_map/dot_general | solution.py:43
  80.7 9.9 %fusion.15 = f32[96,96,128]{2,0,1:T(8,128)} fusion(f32[96,96,128]{2,1,0:T(8,128)S(1)} %convolution_bitcast_fusion.3), kind=kOutput, calls=%fused_computation.27 | convolution fusion | flops 1358991360 | bytes 9437184 | tf_op jit(solution)/shard_map/ab,bxy->axy/dot_general | solution.py:47
  90.7 7.6 %fusion.21 = f32[96,96,128]{2,1,0:T(8,128)S(1)} fusion(f32[96,96,128]{2,0,1:T(8,128)S(1)} %get-tuple-element.21), kind=kOutput, calls=%fused_computation.33 | convolution fusion | flops 1812004864 | bytes 9437184 | tf_op jit(solution)/shard_map/dot_general | solution.py:43
  103.1 9.9 %fusion.19 = f32[96,96,128]{2,0,1:T(8,128)} fusion(f32[96,96,128]{2,1,0:T(8,128)S(1)} %convolution_bitcast_fusion.4), kind=kOutput, calls=%fused_computation.31 | convolution fusion | flops 1358991360 | bytes 9437184 | tf_op jit(solution)/shard_map/ab,bxy->axy/dot_general | solution.py:47
  113.0 7.6 %fusion.25 = f32[96,96,128]{2,1,0:T(8,128)S(1)} fusion(f32[96,96,128]{2,0,1:T(8,128)S(1)} %get-tuple-element.20), kind=kOutput, calls=%fused_computation.37 | convolution fusion | flops 1812004864 | bytes 9437184 | tf_op jit(solution)/shard_map/dot_general | solution.py:43
  120.6 6.1 convolution_bitcast_fusion.6
  126.7 6.3 copy.23
  133.0 9.0 %convolution_bitcast_fusion.2 = f32[96,96,128]{1,0,2:T(8,128)} fusion(f32[96,96,128]{1,0,2:T(8,128)} %copy.23), kind=kOutput, calls=%fused_computation.46 | convolution fusion | flops 1358991360 | bytes 9437184 | tf_op jit(solution)/shard_map/ab,zby->zay/dot_general | solution.py:44
  142.0 6.3 copy.24
  148.3 8.8 %fusion.84 = f32[96,96,128]{2,0,1:T(8,128)} fusion(f32[96,96,128]{2,0,1:T(8,128)} %copy.24), kind=kOutput, calls=%fused_computation.118 | convolution fusion | flops 1358991360 | bytes 9437184 | tf_op jit(solution)/shard_map/ab,bxy->axy/dot_general | solution.py:47
  157.0 15.5 %fusion.8 = (f32[96,1,96,128]{3,0,2,1:T(8,128)S(1)}, f32[96,1,96,128]{3,0,2,1:T(8,128)}, f32[96,1,96,128]{3,0,2,1:T(8,128)}) fusion(f32[96,96,128]{2,0,1:T(8,128)} %copy_convert_fusion), kind=kLoop, calls=%fused_computation.20 | loop fusion | flops 7077888 | bytes 18874368 | tf_op jit(solution)/shard_map/stack | solution.py:57
  172.5 22.2 %fusion.27 = (f32[]{:T(128)}, f32[96,96,128]{2,0,1:T(8,128)}) fusion(f32[96,96,128]{2,0,1:T(8,128)} %fusion.84, f32[96,96,128]{2,0,1:T(8,128)} %fusion.81, f32[96,96,128]{2,0,1:T(8,128)} %fusion.15, f32[96,96,128]{2,0,1:T(8,128)} %fusion.19, bf16[96,96,128]{2,1,0:T(8,128)(2,1)S(1)} %bitcast.111, bf16[1,96,96,128]{3,2,1,0:T(8,128)(2,1)S(1)} %copy-done, ...), kind=kOutput, calls=%fused_computation.43 | convolution fusion | flops 1384943616 | bytes 33030148 | tf_op jit(solution)/shard_map/ab,bxy->axy/dot_general | solution.py:47
  200.0 22.1 %fusion.2 = f32[96,3,96,128]{3,2,1,0:T(8,128)S(1)} fusion(f32[96,3,96,128]{3,0,2,1:T(8,128)S(1)} %maximum_multiply_fusion), kind=kOutput, calls=%fused_computation.10 | convolution fusion | flops 5435965440 | bytes 28311552 | tf_op jit(solution)/shard_map/zcxb,ba->zcxa/dot_general | solution.py:91
  222.1 15.9 %convolution_bitcast_fusion = f32[96,3,96,128]{3,2,1,0:T(8,128)} fusion(f32[96,3,96,128]{3,2,1,0:T(8,128)S(1)} %fusion.2), kind=kOutput, calls=%fused_computation.12 | convolution fusion | flops 4076946432 | bytes 28311552 | tf_op jit(solution)/shard_map/ab,zcby->zcay/dot_general | solution.py:94
  238.0 25.3 %fusion = f32[96,3,96,128]{3,0,2,1:T(8,128)S(1)} fusion(f32[96,3,96,128]{3,2,1,0:T(8,128)} %convolution_bitcast_fusion), kind=kOutput, calls=%fused_computation.8 | convolution fusion | flops 4076946432 | bytes 28311552 | tf_op jit(solution)/shard_map/ab,bcxy->acxy/dot_general | solution.py:99
  263.3 7.1 %pad_maximum_fusion = f32[96,4,96,128]{3,0,2,1:T(8,128)} fusion(f32[96,1,96,128]{3,0,2,1:T(8,128)S(1)} %bitcast.113, f32[96,3,96,128]{3,0,2,1:T(8,128)S(1)} %fusion), kind=kLoop, calls=%fused_computation.6 | loop fusion | flops 4718592 | bytes 37748736 | tf_op jit(solution)/shard_map/concatenate | solution.py:104
  270.4 15.8 %copy.35 = f32[96,4,96,128]{3,2,1,0:T(8,128)} copy(f32[96,4,96,128]{3,0,2,1:T(8,128)} %pad_maximum_fusion) | data formatting | bytes 37748736 | tf_op jit(solution)/shard_map/concatenate | solution.py:104
  286.3 218.0 %reduce-scatter.2.cloned.1.call-done = f32[3,4,96,128]{3,2,1,0:T(8,128)} async-done(((f32[96,4,96,128]{3,2,1,0:T(8,128)}), f32[3,4,96,128]{3,2,1,0:T(8,128)}) %reduce-scatter.2.cloned.1.call-update) | async-done | bytes 589840 | tf_op jit(solution)/shard_map/reduce_scatter | solution.py:103
  504.3 64.7 %psum.31 = f32[]{:T(128)} all-reduce(f32[]{:T(128)} %get-tuple-element.14), channel_id=1, replica_groups=mesh['grp'=4,'sub'=32] {'grp','sub'}, use_global_device_ids=true, to_apply=%region_7.8 | all-reduce | flops 1 | bytes 8 | tf_op jit(solution)/shard_map/psum | solution.py:112
  572.9 79.7 %all-reduce.3 = (f32[]{:T(128)}, f32[]{:T(128)}) all-reduce(f32[]{:T(128)} %multiply_reduce_fusion, f32[]{:T(128)} %multiply_reduce_fusion.1), channel_id=1, replica_groups=mesh['grp'=4,'sub'=32] {'sub'}, use_global_device_ids=true, to_apply=%region_3.4 | all-reduce | flops 2 | bytes 16 | tf_op jit(solution)/shard_map/psum | solution.py:113
  (38 shorter events, 61.5 us)
Async XLA Ops:
  9.8 47.5 %all-to-all-start = ((bf16[32,3,96,128]{3,2,1,0:T(8,128)(2,1)}), bf16[32,3,96,128]{3,2,1,0:T(8,128)(2,1)S(1)}, u32[]{:S(2)}, u32[]{:S(2)}) async-start(bf16[32,3,96,128]{3,2,1,0:T(8,128)(2,1)} %stack.10), calls=%async_computation | async-start | bytes 4718592 | tf_op jit(solution)/shard_map/all_to_all | solution.py:62
  19.4 484.8 %reduce-scatter.2.cloned.1.call-start = ((), (), s32[]{:S(2)}) async-start(), calls=%async_computation.2 | async-start | bytes 19464192 | tf_op jit(solution)/shard_map/reduce_scatter | solution.py:103
  46.9 4.7 copy-start.1
  157.0 15.5 %copy-start = (bf16[1,96,96,128]{3,2,1,0:T(8,128)(2,1)S(1)}, bf16[1,96,96,128]{3,2,1,0:T(8,128)(2,1)}, u32[]{:S(2)}) copy-start(bf16[1,96,96,128]{3,2,1,0:T(8,128)(2,1)} %param.3) | copy-start | bytes 7077892
  172.5 22.3 %copy-start.2 = (f32[96,1,96,128]{3,0,2,1:T(8,128)S(1)}, f32[96,1,96,128]{3,0,2,1:T(8,128)}, u32[]{:S(2)}) copy-start(f32[96,1,96,128]{3,0,2,1:T(8,128)} %get-tuple-element.17) | copy-start | bytes 14155780
  222.1 41.2 %slice-start = ((s8[4718592]{0:T(1024)(128)(4,1)}), s8[4194304]{0:T(1024)(128)(4,1)S(1)}, s32[]{:S(2)}) async-start(s8[4718592]{0:T(1024)(128)(4,1)} %bitcast.112), calls=%async_computation.4 | async-start | bytes 8388608
  238.0 25.3 %slice-start.1 = ((s8[4718592]{0:T(1024)(128)(4,1)}), s8[524288]{0:T(1024)(128)(4,1)S(1)}, s32[]{:S(2)}) async-start(s8[4718592]{0:T(1024)(128)(4,1)} %bitcast.112), calls=%async_computation.5 | async-start | bytes 1048576
  286.2 282.7 %all-reduce.6.cloned.1.call-start = ((), (), s32[]{:S(2)}) async-start(), calls=%async_computation.3 | async-start | bytes 1179648 | tf_op jit(solution)/shard_map/psum | solution.py:106
  654.3 8.4 %collective-permute-start = (f32[1,96,128]{2,1,0:T(8,128)S(1)}, f32[1,96,128]{2,1,0:T(8,128)S(1)}, u32[]{:S(2)}, u32[]{:S(2)}) collective-permute-start(f32[1,96,128]{2,1,0:T(8,128)S(1)} %get-tuple-element.24), channel_id=1, source_target_pairs={{1,0},{2,1},{3,2},{4,3},{5,4},{6,5},{7,6},{8,7},{9,8},{10,9},{11,1... | collective-permute-start | bytes 147464 | tf_op jit(solution)/shard_map/ppermute | solution.py:23
  656.2 10.2 %collective-permute-start.1 = (f32[1,96,128]{2,1,0:T(8,128)S(1)}, f32[1,96,128]{2,1,0:T(8,128)S(1)}, u32[]{:S(2)}, u32[]{:S(2)}) collective-permute-start(f32[1,96,128]{2,1,0:T(8,128)S(1)} %get-tuple-element.25), channel_id=1, source_target_pairs={{0,1},{1,2},{2,3},{3,4},{4,5},{5,6},{6,7},{7,8},{8,9},{9,10},{10,1... | collective-permute-start | bytes 147464 | tf_op jit(solution)/shard_map/ppermute | solution.py:22
Sparse Core Ops, SparseCore 0:
  286.3 217.8 reduce-scatter.1
  506.7 40.8 all-reduce.5
